TPU v7x, 32 devices: a whole 2x2x4 slice. The times are simulated.
32 devices in a mesh: station: 4 (over z), cores: 8 (over y, x, core).
Axes of the slice: x: 2, y: 2, z: 4, core: 2. Of those that a mesh axis runs over, the one named last changes fastest.
Arguments:
- samples: bfloat16 [2, 64, 1048576], P(None, 'station', 'cores'), may hold values from -6 to 6
- delays: int32 [64], P('station'), may hold values from 0 to 32768, as said below
- fringe_rate: int32 [64], P('station'), may hold values from 0 to 4095
- station_of_row: int32 [64], replicated, may hold values from 0 to 63, each once
Outputs:
- visibilities: float32 [65536, 4096], P(('station', 'cores'))
Inputs may be any that keep to these rules, and one draw needn't show every extreme that they name: `delays`: every delay lies between 0 and 32768, and some station's delay is exactly 32768. `station_of_row`: each station number appears once.
All inputs are finite; a program needn't handle non-finite values.
Results may differ from a plain program's by a relative error of at most 0.0035.
Values may be sent and summed in bfloat16 or wider, within the bound.
A program may use at most 640 MiB of HBM per device.

v0:
```python
import math

import jax
import jax.numpy as jnp
from jax import lax
from jax.sharding import PartitionSpec as P

S = 64
NCH = 65536
ROOT = 256
OUTER = 256
MAXD = 32768
PERIOD = 262144


def passed_along(x, axis, by):
    count = lax.axis_size(axis)
    pairs = [(i, i + by) for i in range(count) if 0 <= i + by < count]
    return lax.ppermute(x, axis, pairs)


def dft_tables(length):
    index = jnp.arange(length, dtype=jnp.int32)
    product = index[:, None] * index[None, :] % length
    angle = product.astype(jnp.float32) * (2.0 * math.pi / length)
    return (jnp.cos(angle), -jnp.sin(angle))


def complex_einsum(form, left, right):
    split = lax.Precision.HIGH
    left_real, left_imag = left
    right_real, right_imag = right
    real_out = jnp.einsum(form, left_real, right_real, precision=split) - jnp.einsum(
        form, left_imag, right_imag, precision=split
    )
    imag_out = jnp.einsum(form, left_real, right_imag, precision=split) + jnp.einsum(
        form, left_imag, right_real, precision=split
    )
    return (real_out, imag_out)


def transform(real_in, imag_in):
    local_rows = real_in.shape[0]
    local_segs = real_in.shape[1]
    length = real_in.shape[2]
    shaped = (
        real_in.reshape(local_rows, local_segs, ROOT, OUTER),
        imag_in.reshape(local_rows, local_segs, ROOT, OUTER),
    )
    first_real, first_imag = complex_einsum("rgnm,kn->rgmk", shaped, dft_tables(ROOT))
    outer_index = jnp.arange(OUTER, dtype=jnp.int32)
    inner_index = jnp.arange(ROOT, dtype=jnp.int32)
    twist = (outer_index[:, None] * inner_index[None, :] % length).astype(jnp.float32) * (
        2.0 * math.pi / length
    )
    twist_real = jnp.cos(twist)
    twist_imag = -jnp.sin(twist)
    mixed_real = first_real * twist_real - first_imag * twist_imag
    mixed_imag = first_real * twist_imag + first_imag * twist_real
    second_real, second_imag = complex_einsum(
        "qm,rgmk->qrgk", dft_tables(OUTER), (mixed_real, mixed_imag)
    )
    scale = 1.0 / math.sqrt(length)
    return (second_real * scale, second_imag * scale)


def shards(samples, delays, fringe_rate, station_of_row):
    local_rows = samples.shape[1]
    local_time = samples.shape[2]
    local_segs = local_time // NCH
    head = samples[:, :, :MAXD]
    following = passed_along(head, "cores", -1)
    extended = jnp.concatenate([samples, following], axis=2)

    def align_row(row, delay):
        return lax.dynamic_slice_in_dim(row, delay, local_time, axis=1)

    aligned = jax.vmap(align_row, in_axes=(1, 0), out_axes=1)(extended, delays).astype(jnp.float32)
    moment = (
        lax.axis_index("cores") * local_time + jnp.arange(local_time, dtype=jnp.int32)
    ) % PERIOD
    counter = fringe_rate[:, None] * moment[None, :] % PERIOD
    angle = counter.astype(jnp.float32) * (2.0 * math.pi / PERIOD)
    cosine = jnp.cos(angle)
    sine = jnp.sin(angle)
    rotated_real = (aligned[0] * cosine + aligned[1] * sine).reshape(local_rows, local_segs, NCH)
    rotated_imag = (aligned[1] * cosine - aligned[0] * sine).reshape(local_rows, local_segs, NCH)
    spec_real, spec_imag = transform(rotated_real, rotated_imag)
    spectra = jnp.stack([spec_real, spec_imag], axis=1).astype(jnp.bfloat16)
    selector = (station_of_row[None, :] == jnp.arange(S, dtype=jnp.int32)[:, None]).astype(
        jnp.bfloat16
    )
    arrived = lax.all_to_all(
        spectra[None], ("station", "cores"), split_axis=1, concat_axis=0, tiled=True
    )
    groups = lax.axis_size("station")
    blocks = lax.axis_size("cores")
    arrived = arrived.reshape((groups, blocks) + arrived.shape[1:])
    selector_split = selector.reshape(S, groups, local_rows)
    ordered = jnp.einsum(
        "aAr,ACqprgk->aCqpgk", selector_split, arrived, preferred_element_type=jnp.float32
    ).astype(jnp.bfloat16)
    total_segs = ordered.shape[1] * ordered.shape[4]
    owned_outer = ordered.shape[2]
    inner_len = ordered.shape[5]
    real_in = ordered[:, :, :, 0]
    imag_in = ordered[:, :, :, 1]
    form = "aCqgk,bCqgk->qkab"
    real_out = jnp.einsum(form, real_in, real_in, preferred_element_type=jnp.float32) + jnp.einsum(
        form, imag_in, imag_in, preferred_element_type=jnp.float32
    )
    imag_out = jnp.einsum(form, imag_in, real_in, preferred_element_type=jnp.float32) - jnp.einsum(
        form, real_in, imag_in, preferred_element_type=jnp.float32
    )
    upper = jnp.arange(S)[:, None] <= jnp.arange(S)[None, :]
    packed = jnp.where(upper[None, None], real_out, imag_out) * (1.0 / total_segs)
    return packed.reshape(owned_outer * inner_len, S * S)


def solution(mesh):
    in_specs = (P(None, "station", "cores"), P("station"), P("station"), P())
    out_specs = P(("station", "cores"), None)
    return jax.shard_map(shards, mesh=mesh, in_specs=in_specs, out_specs=out_specs, check_vma=False)
```

profile of v0, /device:TPU:15, one launch (start us, length us, event | category | flops | bytes accessed | tf_op | source)
XLA Modules:
  0.0 1176.4 jit_solution(16152439652469229414)
XLA Ops:
  0.0 15.6 %copy.74 = bf16[2,16,131072]{2,0,1:T(2,128)(2,1)S(1)} copy(bf16[2,16,131072]{2,1,0:T(8,128)(2,1)} %param.4) | data formatting | bytes 16777216 | tf_op args[0]
  31.8 27.0 %maximum_bitcast_fusion = bf16[16,2,163840]{2,1,0:T(2,128)(2,1)} fusion(bf16[2,16,32768]{2,0,1:T(2,128)(2,1)S(1)} %collective-permute-done, bf16[2,16,131072]{2,0,1:T(2,128)(2,1)} %copy-done), kind=kLoop, calls=%fused_computation.14 | loop fusion | flops 20971520 | bytes 20971520 | tf_op jit(solution)/shard_map/vmap()/transpose | solution.py:76
  58.8 68.3 %while.1 = (s32[]{:T(128)}, bf16[16,2,163840]{2,1,0:T(2,128)(2,1)}, s32[16,3]{0,1:T(4,128)S(1)}, bf16[16,2,131072]{2,1,0:T(2,128)(2,1)}, s32[]{:T(128)}) while((s32[]{:T(128)}, bf16[16,2,163840]{2,1,0:T(2,128)(2,1)}, s32[16,3]{0,1:T(4,128)S(1)}, bf16[16,2,131072]{2,1,0:T(2,128)(2,1)}, s32[]{:T(128)}) %tuple.25), condition=%wide.while_cond, body=%wide.while_body.sunk | while | flops 2 | bytes 1050217 | solution.py:76
  134.2 50.3 %slice_reduce_fusion.1 = (f32[16,131072]{1,0:T(8,128)}, f32[16,131072]{1,0:T(8,128)}) fusion(f32[2,16,131072]{2,0,1:T(2,128)S(1)} %convert_bitcast_fusion), kind=kLoop, calls=%fused_computation.19 | loop fusion | bytes 33554432 | tf_op jit(solution)/shard_map/slice | solution.py:86
  221.5 41.8 %fusion.17 = f32[16,2,256,256]{3,2,1,0:T(8,128)S(1)} fusion(f32[16,2,256,256]{2,3,1,0:T(8,128)} %copy.75, f32[16,2,256,256]{2,3,1,0:T(8,128)} %copy.76, s32[2,256,256]{1,2,0:T(8,128)S(1)} %add_select_fusion.1, s32[16]{0:T(128)S(1)} %copy-done.5, f32[256,256,1,1]{1,0,3,2:T(8,128)S(1)} %copy-done.4), kind=kOutput, calls=%fused_computation.51 | convolution fusion | flops 3256877056 | bytes 25952320 | tf_op jit(solution)/shard_map/rgnm,kn->rgmk/dot_general | solution.py:33
  263.4 40.6 %fusion.25 = f32[16,2,256,256]{3,2,1,0:T(8,128)} fusion(f32[16,2,256,256]{2,3,1,0:T(8,128)S(1)} %copy-done.1, f32[16,2,256,256]{2,3,1,0:T(8,128)} %copy.75, s32[2,256,256]{1,2,0:T(8,128)S(1)} %add_select_fusion.1, s32[16]{0:T(128)S(1)} %copy-done.5, f32[256,256,1,1]{1,0,3,2:T(8,128)S(1)} %copy-done.3), kind=kOutput, calls=%fused_computation.59 | convolution fusion | flops 3256877056 | bytes 25952320 | tf_op jit(solution)/shard_map/rgnm,kn->rgmk/dot_general | solution.py:33
  304.0 39.5 %fusion.23 = f32[16,2,256,256]{3,2,1,0:T(8,128)} fusion(f32[16,2,256,256]{2,3,1,0:T(8,128)S(1)} %bitcast.108, f32[16,2,256,256]{2,3,1,0:T(8,128)S(1)} %copy-done.1, s32[2,256,256]{1,2,0:T(8,128)S(1)} %add_select_fusion.1, s32[16]{0:T(128)S(1)} %copy-done.5, f32[256,256,1,1]{1,0,3,2:T(8,128)S(1)} %copy-done.2), kind=kOutput, calls=%fused_computation.57 | convolution fusion | flops 3256877056 | bytes 25952320 | tf_op jit(solution)/shard_map/rgnm,kn->rgmk/dot_general | solution.py:36
  343.5 43.1 %multiply_subtract_fusion = (f32[16,2,256,256]{3,2,1,0:T(8,128)S(1)}, f32[16,2,256,256]{3,2,1,0:T(8,128)S(1)}) fusion(f32[256,256]{1,0:T(8,128)S(1)} %get-tuple-element.29, f32[256,256]{1,0:T(8,128)S(1)} %get-tuple-element.30, f32[16,2,256,256]{3,2,1,0:T(8,128)} %fusion.23, f32[16,2,256,256]{3,2,1,0:T(8,128)} %fusion.25, ...), kind=kOutput, calls=%fused_computation.25 | convolution fusion | flops 3273654272 | bytes 60031040 | tf_op jit(solution)/shard_map/rgnm,kn->rgmk/dot_general | solution.py:36
  413.9 12.0 %fusion.5 = bf16[1,256,1,16,2,256]{5,1,4,3,2,0:T(8,128)(2,1)} fusion(f32[256,16,2,256]{3,0,2,1:T(8,128)} %fusion.19, f32[16,2,256,256]{3,2,1,0:T(8,128)S(1)} %get-tuple-element.25), kind=kOutput, calls=%fused_computation.29 | convolution fusion | flops 3228499968 | bytes 20971520 | tf_op jit(solution)/shard_map/qm,rgmk->qrgk/dot_general | solution.py:36
  432.3 13.4 %copy.79 = bf16[1,256,2,16,2,256]{5,4,3,2,0,1:T(2,128)(2,1)} copy(bf16[1,256,2,16,2,256]{5,1,4,3,2,0:T(8,128)(2,1)} %pad_maximum_fusion) | data formatting | bytes 16777216 | tf_op jit(solution)/shard_map/stack | solution.py:89
  445.7 23.2 %all-to-all-start = ((bf16[1,256,2,16,2,256]{5,4,3,2,0,1:T(2,128)(2,1)}), bf16[1,256,2,16,2,256]{5,4,3,2,0,1:T(2,128)(2,1)}, u32[]{:S(2)}, u32[]{:S(2)}) async-start(bf16[1,256,2,16,2,256]{5,4,3,2,0,1:T(2,128)(2,1)} %copy.79), calls=%async_computation | async-start | bytes 16777216 | tf_op jit(solution)/shard_map/all_to_all | solution.py:93
  469.6 180.1 %all-to-all-done = bf16[1,256,2,16,2,256]{5,4,3,2,0,1:T(2,128)(2,1)} async-done(((bf16[1,256,2,16,2,256]{5,4,3,2,0,1:T(2,128)(2,1)}), bf16[1,256,2,16,2,256]{5,4,3,2,0,1:T(2,128)(2,1)}, u32[]{:S(2)}, u32[]{:S(2)}) %all-to-all-start) | async-done | bytes 8388640 | tf_op jit(solution)/shard_map/all_to_all | solution.py:93
  659.2 11.0 copy.82
  681.1 29.0 %convolution_bitcast_fusion = f32[8,256,64,64]{3,2,1,0:T(8,128)} fusion(bf16[64,8,8,2,256]{0,1,3,4,2:T(8,128)(2,1)} %copy.82, bf16[64,8,8,2,256]{0,1,3,4,2:T(8,128)(2,1)} %copy.84), kind=kOutput, calls=%fused_computation.3 | convolution fusion | flops 268435456 | bytes 41943040 | tf_op jit(solution)/shard_map/aCqgk,bCqgk->qkab/dot_general | solution.py:112
  710.1 29.0 %convolution_bitcast_fusion.1 = f32[8,256,64,64]{3,2,1,0:T(8,128)} fusion(bf16[64,8,8,2,256]{0,1,3,4,2:T(8,128)(2,1)} %copy.84, bf16[64,8,8,2,256]{0,1,3,4,2:T(8,128)(2,1)} %copy.82), kind=kOutput, calls=%fused_computation.4 | convolution fusion | flops 268435456 | bytes 41943040 | tf_op jit(solution)/shard_map/aCqgk,bCqgk->qkab/dot_general | solution.py:112
  739.1 30.0 %convolution_bitcast_fusion.3 = f32[8,256,64,64]{3,2,1,0:T(8,128)} fusion(bf16[64,8,8,2,256]{0,1,3,4,2:T(8,128)(2,1)} %copy.82), kind=kOutput, calls=%fused_computation.6 | convolution fusion | flops 268435456 | bytes 37748736 | tf_op jit(solution)/shard_map/aCqgk,bCqgk->qkab/dot_general | solution.py:109
  769.0 30.1 %convolution_bitcast_fusion.2 = f32[8,256,64,64]{3,2,1,0:T(8,128)} fusion(bf16[64,8,8,2,256]{0,1,3,4,2:T(8,128)(2,1)} %copy.84), kind=kOutput, calls=%fused_computation.5 | convolution fusion | flops 268435456 | bytes 37748736 | tf_op jit(solution)/shard_map/aCqgk,bCqgk->qkab/dot_general | solution.py:109
  799.1 52.1 %copy.93 = f32[8,256,64,64]{1,3,2,0:T(8,128)} copy(f32[8,256,64,64]{3,2,1,0:T(8,128)} %convolution_bitcast_fusion) | data formatting | bytes 67108864 | tf_op jit(solution)/shard_map/aCqgk,bCqgk->qkab/dot_general | solution.py:112
  851.3 52.1 %copy.92 = f32[8,256,64,64]{1,3,2,0:T(8,128)} copy(f32[8,256,64,64]{3,2,1,0:T(8,128)} %convolution_bitcast_fusion.1) | data formatting | bytes 67108864 | tf_op jit(solution)/shard_map/aCqgk,bCqgk->qkab/dot_general | solution.py:112
  903.4 52.1 %copy.86 = f32[8,256,64,64]{1,3,2,0:T(8,128)} copy(f32[8,256,64,64]{3,2,1,0:T(8,128)} %convolution_bitcast_fusion.3) | data formatting | bytes 67108864 | tf_op jit(solution)/shard_map/aCqgk,bCqgk->qkab/dot_general | solution.py:109
  955.5 52.1 %copy.87 = f32[8,256,64,64]{1,3,2,0:T(8,128)} copy(f32[8,256,64,64]{3,2,1,0:T(8,128)} %convolution_bitcast_fusion.2) | data formatting | bytes 67108864 | tf_op jit(solution)/shard_map/aCqgk,bCqgk->qkab/dot_general | solution.py:109
  1007.6 54.7 %select_multiply_fusion = f32[8,256,64,64]{1,3,2,0:T(8,128)} fusion(f32[8,256,64,64]{1,3,2,0:T(8,128)} %copy.92, f32[8,256,64,64]{1,3,2,0:T(8,128)} %copy.93, f32[8,256,64,64]{1,3,2,0:T(8,128)} %copy.86, f32[8,256,64,64]{1,3,2,0:T(8,128)} %copy.87, pred[64,64]{1,0:T(8,128)(4,1)S(1)} %copy-done.6), kind=kLoop, calls=%fused_computation.2 | loop fusion | flops 33554432 | bytes 167776256 | tf_op jit(solution)/shard_map/mul | solution.py:116
  1062.3 58.9 %copy.106 = f32[8,256,64,64]{3,2,1,0:T(8,128)} copy(f32[8,256,64,64]{1,3,2,0:T(8,128)} %select_multiply_fusion) | data formatting | bytes 67108864 | tf_op jit(solution)/shard_map/reshape | solution.py:117
  1121.2 54.7 %reshape.188 = f32[2048,4096]{1,0:T(8,128)} reshape(f32[8,256,64,64]{3,2,1,0:T(8,128)} %copy.106) | data formatting | bytes 67108864 | tf_op jit(solution)/shard_map/reshape | solution.py:117
  (98 shorter events, 183.3 us)
Async XLA Ops:
  0.0 24.5 %copy-start.8 = (s32[16]{0:T(128)S(1)}, s32[16]{0:T(128)}, u32[]{:S(2)}) copy-start(s32[16]{0:T(128)} %param.5) | copy-start | bytes 196
  15.6 3.2 copy-start
  21.7 10.0 collective-permute-start
  212.1 9.3 copy-start.4
  212.1 9.3 copy-start.5
  221.5 41.9 %copy-start.1 = (f32[16,2,256,256]{2,3,1,0:T(8,128)S(1)}, f32[16,2,256,256]{2,3,1,0:T(8,128)}, u32[]{:S(2)}) copy-start(f32[16,2,256,256]{2,3,1,0:T(8,128)} %copy.76) | copy-start | bytes 25165828
  221.5 41.9 %copy-start.3 = (f32[256,256,1,1]{1,0,3,2:T(8,128)S(1)}, f32[256,256,1,1]{1,0,3,2:T(8,128)}, u32[]{:S(2)}) copy-start(f32[256,256,1,1]{1,0,3,2:T(8,128)} %fusion.107) | copy-start | bytes 786436
  221.5 82.5 %slice-start = ((s8[8388608]{0:T(1024)(128)(4,1)}), s8[4194304]{0:T(1024)(128)(4,1)S(1)}, s32[]{:S(2)}) async-start(s8[8388608]{0:T(1024)(128)(4,1)} %bitcast.107), calls=%async_computation.1 | async-start | bytes 8388608
  263.3 40.6 %slice-start.1 = ((s8[8388608]{0:T(1024)(128)(4,1)}), s8[4194304]{0:T(1024)(128)(4,1)S(1)}, s32[]{:S(2)}) async-start(s8[8388608]{0:T(1024)(128)(4,1)} %bitcast.107), calls=%async_computation.2 | async-start | bytes 8388608
  263.4 40.6 %copy-start.2 = (f32[256,256,1,1]{1,0,3,2:T(8,128)S(1)}, f32[256,256,1,1]{1,0,3,2:T(8,128)}, u32[]{:S(2)}) copy-start(f32[256,256,1,1]{1,0,3,2:T(8,128)} %fusion.105) | copy-start | bytes 786436
  445.7 23.2 %copy-start.7 = (s32[64]{0:T(128)S(1)}, s32[64]{0:T(128)}, u32[]{:S(2)}) copy-start(s32[64]{0:T(128)} %param.7) | copy-start | bytes 772
  445.7 204.0 %all-to-all-start = ((bf16[1,256,2,16,2,256]{5,4,3,2,0,1:T(2,128)(2,1)}), bf16[1,256,2,16,2,256]{5,4,3,2,0,1:T(2,128)(2,1)}, u32[]{:S(2)}, u32[]{:S(2)}) async-start(bf16[1,256,2,16,2,256]{5,4,3,2,0,1:T(2,128)(2,1)} %copy.79), calls=%async_computation | async-start | bytes 16777216 | tf_op jit(solution)/shard_map/all_to_all | solution.py:93
  955.5 52.1 %copy-start.6 = (pred[64,64]{1,0:T(8,128)(4,1)S(1)}, pred[64,64]{1,0:T(8,128)(4,1)}, u32[]{:S(2)}) copy-start(pred[64,64]{1,0:T(8,128)(4,1)} %iota_compare_fusion.1) | copy-start | bytes 12292
where the time goes:
time: 1200 us; the launch traced here: 1180 us
  local copies, waits for them, and re-layouts  538 us (45%)
  matrix products  328 us (27%)
  waiting for transfers between devices  180 us (15%)
  other arithmetic  103 us (9%)
  starting transfers between devices  25.9 us (2%)
    all_to_all x1, waiting for transfers between devices, shards(): lax.all_to_all(spectra[None], ('station', 'cores'), split_axis=1, concat_...  180 us
    reshape x2, local copies, waits for them, and re-layouts, shards(): return packed.reshape(owned_outer * inner_len, S * S)  114 us
    gather x48, local copies, waits for them, and re-layouts  68.2 us
    mul x1, other arithmetic, shards(): jnp.where(upper[None, None], real_out, imag_out) * (1.0 / total_segs)  54.7 us
    dot_general x2, matrix products, complex_einsum(): jnp.einsum(form, left_imag, right_imag, precision=split)  52.4 us
    dot_general x1, local copies, waits for them, and re-layouts, shards(): jnp.einsum(form, imag_in, imag_in, preferred_element_type=jnp.float32)  52.1 us
    dot_general x1, local copies, waits for them, and re-layouts, shards(): jnp.einsum(form, real_in, real_in, preferred_element_type=jnp.float32)  52.1 us
    dot_general x1, local copies, waits for them, and re-layouts, shards(): jnp.einsum(form, real_in, imag_in, preferred_element_type=jnp.float32)  52.1 us
  transfers between devices with their start and end apart: 2, of which 1 were waited for; matrix products, arithmetic and copies ran while one was open for 1% of the time, Pallas kernels for 0%

commit v1 on v0

v1 whole, which is shorter than its diff:
```python
import functools
import math

import jax
import jax.numpy as jnp
import numpy as np
from jax import lax
from jax.experimental import pallas as pl
from jax.experimental.pallas import tpu as pltpu
from jax.sharding import PartitionSpec as P

S = 64
NCH = 65536
ROOT = 256
MAXD = 32768
PERIOD = 262144
F32 = jnp.float32
BF16 = jnp.bfloat16


def passed_along(x, axis, by):
    count = lax.axis_size(axis)
    pairs = [(i, i + by) for i in range(count) if 0 <= i + by < count]
    return lax.ppermute(x, axis, pairs)


def dft_table(length, scale):
    index = np.arange(ROOT)
    angle = (index[:, None] * index[None, :] % length) * (2.0 * math.pi / length)
    return np.stack([np.cos(angle) * scale, -np.sin(angle) * scale]).astype(np.float32)


def halves(x):
    high = x.astype(BF16)
    return high, (x - high.astype(F32)).astype(BF16)


def block_form(real, imag):
    return jnp.concatenate(
        [jnp.concatenate([real, -imag], axis=1), jnp.concatenate([imag, real], axis=1)], axis=0
    )


def dot(a, b, dims=((1,), (0,))):
    return lax.dot_general(a, b, (dims, ((), ())), preferred_element_type=F32)


def phases(counter):
    angle = (counter % PERIOD).astype(F32) * (2.0 * math.pi / PERIOD)
    return jnp.stack([jnp.cos(angle), -jnp.sin(angle)], axis=-2)


def front_kernel(segs, delays, x_ref, follow_ref, u_ref, v_ref, f_ref, tw_ref, gh_ref, gl_ref, o_ref, ext):
    r = pl.program_id(0)
    here = x_ref.shape[2]
    after = follow_ref.shape[2]
    for p in range(2):
        for h in range(2):
            cols = slice(h * 128, h * 128 + 128)
            ext[p, h, :here] = x_ref[p, 0, :, cols].astype(F32)
            ext[p, h, here : here + after] = follow_ref[p, 0, :, cols].astype(F32)
    delay = delays[r]
    down = delay // ROOT
    across = delay % ROOT
    u_real, u_imag = u_ref[0, 0:1], u_ref[0, 1:2]
    f_real, f_imag = f_ref[0], f_ref[1]
    fh_real, fl_real = halves(f_real * u_real - f_imag * u_imag)
    fh_imag, fl_imag = halves(f_real * u_imag + f_imag * u_real)
    f_high = block_form(fh_real, fh_imag)
    f_low = block_form(fl_real, fl_imag)
    lane = lax.broadcasted_iota(jnp.int32, (ROOT, ROOT), 1)
    kept = lane >= across
    for s in range(segs):
        parts = []
        for p in range(2):
            begin = down + s * ROOT
            first = jnp.concatenate([ext[p, h, pl.ds(begin, ROOT), :] for h in range(2)], axis=1)
            second = jnp.concatenate([ext[p, h, pl.ds(begin + 1, ROOT), :] for h in range(2)], axis=1)
            parts.append(pltpu.roll(jnp.where(kept, first, second), ROOT - across, 1).astype(BF16))
        x = jnp.concatenate(parts, axis=0)
        y = dot(f_high, x) + dot(f_low, x)
        y_real, y_imag = y[:ROOT], y[ROOT:]
        v_real, v_imag = v_ref[0, s, 0:1], v_ref[0, s, 1:2]
        t_real = tw_ref[0] * v_real - tw_ref[1] * v_imag
        t_imag = tw_ref[0] * v_imag + tw_ref[1] * v_real
        mh_real, ml_real = halves(y_real * t_real - y_imag * t_imag)
        mh_imag, ml_imag = halves(y_real * t_imag + y_imag * t_real)
        high = jnp.concatenate([mh_real, mh_imag], axis=1)
        low = jnp.concatenate([ml_real, ml_imag], axis=1)
        rows = ((1,), (1,))
        z = dot(gh_ref[...], high, rows) + dot(gh_ref[...], low, rows) + dot(gl_ref[...], high, rows)
        z = z.astype(BF16)
        for p in range(2):
            o_ref[:, p, s, 0] = z[p * ROOT : (p + 1) * ROOT].reshape(o_ref.shape[0], o_ref.shape[4], ROOT)


def front(samples, following, delays, u, v, owners):
    _, local_rows, here, _ = samples.shape
    after = following.shape[2]
    segs = here // ROOT
    owned = ROOT // owners
    table = dft_table(ROOT, 1.0)
    gh, gl = halves(block_form(jnp.asarray(table[0]), jnp.asarray(table[1])))
    whole3 = pl.BlockSpec((2, ROOT, ROOT), lambda r, d: (0, 0, 0))
    whole2 = pl.BlockSpec((2 * ROOT, 2 * ROOT), lambda r, d: (0, 0))
    return pl.pallas_call(
        functools.partial(front_kernel, segs),
        grid_spec=pltpu.PrefetchScalarGridSpec(
            num_scalar_prefetch=1,
            grid=(local_rows,),
            in_specs=[
                pl.BlockSpec((2, 1, here, ROOT), lambda r, d: (0, r, 0, 0)),
                pl.BlockSpec((2, 1, after, ROOT), lambda r, d: (0, r, 0, 0)),
                pl.BlockSpec((1, 2, ROOT), lambda r, d: (r, 0, 0)),
                pl.BlockSpec((1, segs, 2, ROOT), lambda r, d: (r, 0, 0, 0)),
                whole3,
                whole3,
                whole2,
                whole2,
            ],
            out_specs=pl.BlockSpec((owners, 2, segs, 1, owned, ROOT), lambda r, d: (0, 0, 0, r, 0, 0)),
            scratch_shapes=[
                pltpu.VMEM((2, 2, here + after + 8, 128), F32),
            ],
        ),
        out_shape=jax.ShapeDtypeStruct((owners, 2, segs, local_rows, owned, ROOT), BF16),
        compiler_params=pltpu.CompilerParams(vmem_limit_bytes=56 * 1024 * 1024),
        name="front",
    )(delays, samples, following, u, v, jnp.asarray(table), jnp.asarray(dft_table(NCH, 1.0 / 256.0)), gh, gl)


def cross_kernel(total_segs, x_ref, sel_ref, o_ref, wide, packed):
    for g in range(total_segs):
        t = dot(x_ref[0, g], sel_ref[...], ((0,), (0,)))
        wide[pl.ds(2 * g * ROOT, ROOT), :] = t[:, :128]
        wide[pl.ds((2 * g + 1) * ROOT, ROOT), :] = t[:, 128:]
    a = lax.broadcasted_iota(jnp.int32, (S, 128), 0)
    lane = lax.broadcasted_iota(jnp.int32, (S, 128), 1)
    straight = jnp.where(lane < S, lane - a, a - lane + S - 1) >= 0
    left = lax.broadcasted_iota(jnp.int32, (8, 128), 1) < S

    @pl.loop(0, ROOT // 8)
    def _(block):
        for c in range(8):
            w = wide[pl.ds(block * 8 + c, 2 * total_segs, stride=ROOT), :].astype(BF16)
            out = dot(w[:, :S], w, ((0,), (0,))) * (1.0 / total_segs)
            packed[c * S : (c + 1) * S, :] = jnp.where(straight, out, pltpu.roll(out, S, 1))
        for j in range(S // 2):
            even = packed[pl.ds(2 * j, 8, stride=S), :]
            odd = packed[pl.ds(2 * j + 1, 8, stride=S), :]
            o_ref[pl.ds(pl.multiple_of(block * 8, 8), 8), j * 128 : (j + 1) * 128] = jnp.where(left, even, odd)


def cross(x, sel):
    owned, total_segs = x.shape[0], x.shape[1]
    return pl.pallas_call(
        functools.partial(cross_kernel, total_segs),
        grid=(owned,),
        in_specs=[
            pl.BlockSpec((1, total_segs, 2 * S, ROOT), lambda q: (q, 0, 0, 0)),
            pl.BlockSpec((2 * S, 4 * S), lambda q: (0, 0)),
        ],
        out_specs=pl.BlockSpec((ROOT, S * S), lambda q: (q, 0)),
        out_shape=jax.ShapeDtypeStruct((owned * ROOT, S * S), F32),
        scratch_shapes=[
            pltpu.VMEM((2 * total_segs * ROOT, 128), F32),
            pltpu.VMEM((8 * S, 128), F32),
        ],
        compiler_params=pltpu.CompilerParams(vmem_limit_bytes=56 * 1024 * 1024),
        name="cross",
    )(x, sel)


def shards(samples, delays, fringe_rate, station_of_row):
    _, local_rows, local_time = samples.shape
    segs = local_time // NCH
    groups = lax.axis_size("station")
    blocks = lax.axis_size("cores")
    owners = groups * blocks
    head = samples[:, :, :MAXD].reshape(2, local_rows, MAXD // ROOT, ROOT)
    following = passed_along(head, "cores", -1)
    shaped = samples.reshape(2, local_rows, local_time // ROOT, ROOT)
    index = jnp.arange(ROOT, dtype=jnp.int32)
    u = phases(fringe_rate[:, None] * (ROOT * index)[None, :])
    start = (lax.axis_index("cores") * segs + jnp.arange(segs, dtype=jnp.int32)) * NCH % PERIOD
    v = phases(fringe_rate[:, None, None] * (start[:, None] + index[None, :])[None])
    spectra = front(shaped, following, delays, u, v, owners)
    arrived = lax.all_to_all(spectra, ("station", "cores"), split_axis=0, concat_axis=0, tiled=True)
    owned = arrived.shape[4]
    arrived = arrived.reshape(groups, blocks, 2, segs, local_rows, owned, ROOT)
    ordered = arrived.transpose(5, 1, 3, 2, 0, 4, 6).reshape(owned, blocks * segs, 2 * S, ROOT)
    pick = (station_of_row[:, None] == jnp.arange(S, dtype=jnp.int32)[None, :]).astype(BF16)
    none = jnp.zeros_like(pick)
    sel = jnp.concatenate(
        [
            jnp.concatenate([pick, none, none, pick], axis=1),
            jnp.concatenate([none, -pick, pick, none], axis=1),
        ],
        axis=0,
    )
    return cross(ordered, sel)


def solution(mesh):
    in_specs = (P(None, "station", "cores"), P("station"), P("station"), P())
    out_specs = P(("station", "cores"), None)
    return jax.shard_map(shards, mesh=mesh, in_specs=in_specs, out_specs=out_specs, check_vma=False)
```

time: 1200 us -> 417 us (0.35); the launches traced: 1180 us -> 410 us
  local copies, waits for them, and re-layouts: 538 us -> 22.4 us
  matrix products: 328 us -> 0 us
  Pallas kernels: 0 us -> 183 us
  other arithmetic: 103 us -> 3.91 us
    dot_general x13 -> x0, matrix products: 328 us -> none  [the longest x2 52.4 us: complex_einsum(): jnp.einsum(form, left_imag, right_imag, precision=split)]
    dot_general x4 -> x0, local copies, waits for them, and re-layouts: 208 us -> none  [the longest x1 52.1 us: shards(): jnp.einsum(form, imag_in, imag_in, preferred_element_type=jnp.float32)]
    pallas_call x0 -> x2, Pallas kernels: none -> 183 us  [the longest x1 134 us: cross(): pl.pallas_call(functools.partial(cross_kernel, total_segs), grid=(owned,)...]
    reshape x2 -> x1, local copies, waits for them, and re-layouts: 114 us -> 8.65 us  [shards(): arrived = arrived.reshape(groups, blocks, 2, segs, local_rows, owned, ROOT)]
    gather x48 -> x0, local copies, waits for them, and re-layouts: 68.2 us -> none
    mul x1, other arithmetic: 54.7 us -> 0.01 us  [shards(): u = phases(fringe_rate[:, None] * (ROOT * index)[None, :])]
    slice x2 -> x1, local copies, waits for them, and re-layouts: 53.2 us -> 1.73 us  [shards(): head = samples[:, :, :MAXD].reshape(2, local_rows, MAXD // ROOT, ROOT)]
    squeeze x5 -> x0, local copies, waits for them, and re-layouts: 44.3 us -> none  [the longest x2 14.6 us: shards(): real_in = ordered[:, :, :, 0]]
  transfers between devices with their start and end apart: 2 -> 2, of which waited for: 1 -> 1; matrix products, arithmetic and copies ran while one was open for 1% -> 3% of each run, Pallas kernels for 0% -> 0%
where the time goes in v1:
time: 417 us; the launch traced here: 410 us
  Pallas kernels  183 us (44%)
  waiting for transfers between devices  180 us (43%)
  local copies, waits for them, and re-layouts  22.4 us (5%)
  starting transfers between devices  21.4 us (5%)
    all_to_all x1, waiting for transfers between devices, shards(): lax.all_to_all(spectra, ('station', 'cores'), split_axis=0, concat_axis=0...  180 us
    pallas_call x1, Pallas kernels, cross(): pl.pallas_call(functools.partial(cross_kernel, total_segs), grid=(owned,)...  134 us
    pallas_call x1, Pallas kernels, front(): pl.pallas_call(functools.partial(front_kernel, segs), grid_spec=pltpu.Pre...  48.9 us
    all_to_all x1, starting transfers between devices, shards(): lax.all_to_all(spectra, ('station', 'cores'), split_axis=0, concat_axis=0...  18.7 us
    unnamed x8, local copies, waits for them, and re-layouts  12 us
    reshape x1, local copies, waits for them, and re-layouts, shards(): arrived = arrived.reshape(groups, blocks, 2, segs, local_rows, owned, ROOT)  8.65 us
  transfers between devices with their start and end apart: 2, of which 1 were waited for; matrix products, arithmetic and copies ran while one was open for 3% of the time, Pallas kernels for 0%

profile of v1, /device:TPU:15, one launch (start us, length us, event | category | flops | bytes accessed | tf_op | source)
XLA Modules:
  0.0 410.3 jit_solution(4189416213013967401)
XLA Ops:
  0.0 1.7 slice.3
  1.7 1.8 copy.14
  3.6 2.7 collective-permute-start
  6.3 0.0 copy-start.1
  6.3 8.8 %copy.13 = bf16[4,8,512,256]{3,2,1,0:T(8,128)(2,1)} copy(bf16[4,8,512,256]{3,1,2,0:T(8,128)(2,1)} %bitcast.14) | data formatting | bytes 16777216
  15.1 0.0 copy-done.1
  15.1 0.1 fusion.3
  15.2 0.5 fusion.7
  15.7 0.6 pad_maximum_fusion.1.u_ref
  16.3 0.1 iota_add_fusion
  16.4 0.1 fusion
  16.5 1.0 fusion.6
  17.5 0.7 pad_maximum_fusion.v_ref
  18.2 0.0 collective-permute-done.follow_ref
  18.2 1.4 copy-done
  19.5 48.9 %front.1 = bf16[32,2,2,16,8,256]{5,4,3,2,1,0:T(8,128)(2,1)} custom-call(s32[16]{0:T(128)} %delays.1, bf16[2,16,512,256]{3,2,1,0:T(8,128)(2,1)} %bitcast.13, bf16[2,16,128,256]{3,2,1,0:T(8,128)(2,1)} %copy-done, f32[16,2,256]{2,1,0:T(2,128)} %pad_maximum_fusion.1.u_ref, f32[16,2,2,256]{3,2,1,0:T(2,128)} %pad_maximum_fusion.v_ref, ...), custom_call_target="tpu_custom_call" | custom-call | tf_op jit(solution)/shard_map/front/pallas_call | solution.py:106
  68.5 18.7 %all-to-all-start = ((bf16[32,2,2,16,8,256]{5,4,3,2,1,0:T(8,128)(2,1)}), bf16[32,2,2,16,8,256]{5,4,3,2,1,0:T(8,128)(2,1)}, u32[]{:S(2)}, u32[]{:S(2)}) async-start(bf16[32,2,2,16,8,256]{5,4,3,2,1,0:T(8,128)(2,1)} %front.1), calls=%async_computation | async-start | bytes 16777216 | tf_op jit(solution)/shard_map/all_to_all | solution.py:188
  87.1 0.0 copy-done.2
  87.1 0.1 fusion.5
  87.2 0.1 fusion.2
  87.3 0.7 maximum_maximum_fusion.sel_ref
  88.0 179.9 %all-to-all-done = bf16[32,2,2,16,8,256]{5,4,3,2,1,0:T(8,128)(2,1)} async-done(((bf16[32,2,2,16,8,256]{5,4,3,2,1,0:T(8,128)(2,1)}), bf16[32,2,2,16,8,256]{5,4,3,2,1,0:T(8,128)(2,1)}, u32[]{:S(2)}, u32[]{:S(2)}) %all-to-all-start) | async-done | bytes 8388640 | tf_op jit(solution)/shard_map/all_to_all | solution.py:188
  267.9 8.7 %copy.12 = bf16[4,8,2,2,16,8,256]{6,4,0,2,3,1,5:T(8,128)(2,1)} copy(bf16[4,8,2,2,16,8,256]{6,5,4,3,2,1,0:T(8,128)(2,1)} %bitcast) | data formatting | bytes 16777216 | tf_op jit(solution)/shard_map/reshape | solution.py:190
  276.6 133.7 %cross.1 = f32[2048,4096]{1,0:T(8,128)} custom-call(bf16[8,16,128,256]{3,2,1,0:T(8,128)(2,1)} %bitcast.12, bf16[128,256]{1,0:T(8,128)(2,1)} %maximum_maximum_fusion.sel_ref), custom_call_target="tpu_custom_call" | custom-call | tf_op jit(solution)/shard_map/cross/pallas_call | solution.py:156
  (6 shorter events, 0.0 us)
Async XLA Ops:
  3.6 14.6 %collective-permute-start = (bf16[2,16,128,256]{3,2,1,0:T(8,128)(2,1)}, bf16[2,16,128,256]{3,2,1,0:T(8,128)(2,1)S(1)}, u32[]{:S(2)}, u32[]{:S(2)}) collective-permute-start(bf16[2,16,128,256]{3,2,1,0:T(8,128)(2,1)} %bitcast.11), channel_id=1, source_target_pairs={{1,0},{2,1},{3,2},{4,3},{5,4},{6,5},{7,6},{9,8},{10,9},{11,10},{12... | collective-permute-start | bytes 6291464 | tf_op jit(solution)/shard_map/ppermute | solution.py:24
  6.3 8.8 %copy-start.1 = (s32[16]{0:T(128)S(1)}, s32[16]{0:T(128)}, u32[]{:S(2)}) copy-start(s32[16]{0:T(128)} %param.10) | copy-start | bytes 196
  18.2 1.4 copy-start
  68.5 18.7 %copy-start.2 = (s32[64]{0:T(128)S(1)}, s32[64]{0:T(128)}, u32[]{:S(2)}) copy-start(s32[64]{0:T(128)} %param.11) | copy-start | bytes 772
  68.5 199.5 %all-to-all-start = ((bf16[32,2,2,16,8,256]{5,4,3,2,1,0:T(8,128)(2,1)}), bf16[32,2,2,16,8,256]{5,4,3,2,1,0:T(8,128)(2,1)}, u32[]{:S(2)}, u32[]{:S(2)}) async-start(bf16[32,2,2,16,8,256]{5,4,3,2,1,0:T(8,128)(2,1)} %front.1), calls=%async_computation | async-start | bytes 16777216 | tf_op jit(solution)/shard_map/all_to_all | solution.py:188

commit v2 on v1

--- a/solution.py
+++ b/solution.py
@@ -129,9 +129,73 @@
     )(delays, samples, following, u, v, jnp.asarray(table), jnp.asarray(dft_table(NCH, 1.0 / 256.0)), gh, gl)
 
 
-def cross_kernel(total_segs, x_ref, sel_ref, o_ref, wide, packed):
+def cross_kernel(groups, blocks, segs, local_rows, x_ref, sel_ref, o_ref, recv, wide, packed, send_sem, recv_sem, own_sem):
+    q = pl.program_id(0)
+    count = pl.num_programs(0)
+    owners = groups * blocks
+    total_segs = blocks * segs
+    me = lax.axis_index("station") * blocks + lax.axis_index("cores")
+
+    def coords(d):
+        return {"station": d // blocks, "cores": lax.rem(d, blocks)}
+
+    def remote(step, i):
+        dest = lax.rem(me + i, owners)
+        return pltpu.make_async_remote_copy(
+            src_ref=x_ref.at[step, dest],
+            dst_ref=recv.at[step, me],
+            send_sem=send_sem.at[step],
+            recv_sem=recv_sem.at[step],
+            device_id=coords(dest),
+            device_id_type=pl.DeviceIdType.MESH,
+        )
+
+    def own(step):
+        return pltpu.make_async_copy(x_ref.at[step, me], recv.at[step, me], own_sem.at[step])
+
+    @pl.when(q == 0)
+    def _():
+        barrier = pltpu.get_barrier_semaphore()
+
+        @pl.loop(1, owners)
+        def _(i):
+            pl.semaphore_signal(
+                barrier, inc=1, device_id=coords(lax.rem(me + i, owners)), device_id_type=pl.DeviceIdType.MESH
+            )
+
+        pl.semaphore_wait(barrier, owners - 1)
+
+        @pl.loop(0, x_ref.shape[0])
+        def _(step):
+            own(step).start()
+
+            @pl.loop(1, owners)
+            def _(i):
+                remote(step, i).start()
+
+    own(q).wait()
+
+    others = recv.at[q, pl.ds(0, owners - 1)]
+    pltpu.make_async_copy(others, others, recv_sem.at[q]).wait()
+
+    @pl.when(q == count - 1)
+    def _():
+        @pl.loop(0, x_ref.shape[0])
+        def _(step):
+            gone = recv.at[step, pl.ds(0, owners - 1)]
+            pltpu.make_async_copy(gone, gone, send_sem.at[step]).wait()
+
     for g in range(total_segs):
-        t = dot(x_ref[0, g], sel_ref[...], ((0,), (0,)))
+        c, s = g // segs, g % segs
+        x = jnp.concatenate(
+            [
+                recv[q, st * blocks + c, (p * segs + s) * local_rows : (p * segs + s + 1) * local_rows, :]
+                for p in range(2)
+                for st in range(groups)
+            ],
+            axis=0,
+        )
+        t = dot(x, sel_ref[...], ((0,), (0,)))
         wide[pl.ds(2 * g * ROOT, ROOT), :] = t[:, :128]
         wide[pl.ds((2 * g + 1) * ROOT, ROOT), :] = t[:, 128:]
     a = lax.broadcasted_iota(jnp.int32, (S, 128), 0)
@@ -151,22 +215,29 @@
             o_ref[pl.ds(pl.multiple_of(block * 8, 8), 8), j * 128 : (j + 1) * 128] = jnp.where(left, even, odd)
 
 
-def cross(x, sel):
-    owned, total_segs = x.shape[0], x.shape[1]
+def cross(x, sel, groups, blocks, segs, local_rows):
+    owned = x.shape[0]
+    total_segs = blocks * segs
     return pl.pallas_call(
-        functools.partial(cross_kernel, total_segs),
+        functools.partial(cross_kernel, groups, blocks, segs, local_rows),
         grid=(owned,),
         in_specs=[
-            pl.BlockSpec((1, total_segs, 2 * S, ROOT), lambda q: (q, 0, 0, 0)),
+            pl.BlockSpec(memory_space=pl.ANY),
             pl.BlockSpec((2 * S, 4 * S), lambda q: (0, 0)),
         ],
         out_specs=pl.BlockSpec((ROOT, S * S), lambda q: (q, 0)),
         out_shape=jax.ShapeDtypeStruct((owned * ROOT, S * S), F32),
         scratch_shapes=[
+            pltpu.VMEM(x.shape, BF16),
             pltpu.VMEM((2 * total_segs * ROOT, 128), F32),
             pltpu.VMEM((8 * S, 128), F32),
+            pltpu.SemaphoreType.DMA((owned,)),
+            pltpu.SemaphoreType.DMA((owned,)),
+            pltpu.SemaphoreType.DMA((owned,)),
         ],
-        compiler_params=pltpu.CompilerParams(vmem_limit_bytes=56 * 1024 * 1024),
+        compiler_params=pltpu.CompilerParams(
+            vmem_limit_bytes=48 * 1024 * 1024, collective_id=0, has_side_effects=True
+        ),
         name="cross",
     )(x, sel)
 
@@ -185,10 +256,8 @@
     start = (lax.axis_index("cores") * segs + jnp.arange(segs, dtype=jnp.int32)) * NCH % PERIOD
     v = phases(fringe_rate[:, None, None] * (start[:, None] + index[None, :])[None])
     spectra = front(shaped, following, delays, u, v, owners)
-    arrived = lax.all_to_all(spectra, ("station", "cores"), split_axis=0, concat_axis=0, tiled=True)
-    owned = arrived.shape[4]
-    arrived = arrived.reshape(groups, blocks, 2, segs, local_rows, owned, ROOT)
-    ordered = arrived.transpose(5, 1, 3, 2, 0, 4, 6).reshape(owned, blocks * segs, 2 * S, ROOT)
+    owned = spectra.shape[4]
+    sent = spectra.transpose(4, 0, 1, 2, 3, 5).reshape(owned, owners, 2 * segs * local_rows, ROOT)
     pick = (station_of_row[:, None] == jnp.arange(S, dtype=jnp.int32)[None, :]).astype(BF16)
     none = jnp.zeros_like(pick)
     sel = jnp.concatenate(
@@ -198,7 +267,7 @@
         ],
         axis=0,
     )
-    return cross(ordered, sel)
+    return cross(sent, sel, groups, blocks, segs, local_rows)
 
 
 def solution(mesh):

time: 417 us -> 339 us (0.81); the launches traced: 410 us -> 338 us
  waiting for transfers between devices: 180 us -> 0.01 us
  Pallas kernels: 183 us -> 287 us
  local copies, waits for them, and re-layouts: 22.4 us -> 45.6 us
  starting transfers between devices: 21.4 us -> 2.7 us
    all_to_all x1 -> x0, waiting for transfers between devices: 180 us -> none  [shards(): lax.all_to_all(spectra, ('station', 'cores'), split_axis=0, concat_axis=0...]
    pallas_call x1, Pallas kernels: 134 us -> 238 us  [cross(): pl.pallas_call(functools.partial(cross_kernel, groups, blocks, segs, loca...]
    unnamed x8 -> x9, local copies, waits for them, and re-layouts: 12 us -> 35 us
    all_to_all x1 -> x0, starting transfers between devices: 18.7 us -> none  [shards(): lax.all_to_all(spectra, ('station', 'cores'), split_axis=0, concat_axis=0...]
    transpose x0 -> x1, local copies, waits for them, and re-layouts: none -> 8.82 us  [shards(): spectra.transpose(4, 0, 1, 2, 3, 5)]
    reshape x1 -> x0, local copies, waits for them, and re-layouts: 8.65 us -> none  [shards(): arrived = arrived.reshape(groups, blocks, 2, segs, local_rows, owned, ROOT)]
  transfers between devices with their start and end apart: 2 -> 1, of which waited for: 1 -> 0; matrix products, arithmetic and copies ran while one was open for 3% -> 4% of each run, Pallas kernels for 0% -> 0%
where the time goes in v2:
time: 339 us; the launch traced here: 338 us
  Pallas kernels  287 us (85%)
  local copies, waits for them, and re-layouts  45.6 us (13%)
    pallas_call x1, Pallas kernels, cross(): pl.pallas_call(functools.partial(cross_kernel, groups, blocks, segs, loca...  238 us
    pallas_call x1, Pallas kernels, front(): pl.pallas_call(functools.partial(front_kernel, segs), grid_spec=pltpu.Pre...  48.9 us
    unnamed x9, local copies, waits for them, and re-layouts  35 us
    transpose x1, local copies, waits for them, and re-layouts, shards(): spectra.transpose(4, 0, 1, 2, 3, 5)  8.82 us
  transfers between devices with their start and end apart: 1, of which 0 were waited for; matrix products, arithmetic and copies ran while one was open for 4% of the time, Pallas kernels for 0%

profile of v2, /device:TPU:15, one launch (start us, length us, event | category | flops | bytes accessed | tf_op | source)
XLA Modules:
  0.0 338.4 jit_solution(3913770826383125139)
XLA Ops:
  0.0 1.7 slice.3
  1.7 1.8 copy.14
  3.6 2.7 collective-permute-start
  6.3 0.0 copy-start.1
  6.3 0.0 copy-start.2
  6.3 8.8 %copy.13 = bf16[4,8,512,256]{3,2,1,0:T(8,128)(2,1)} copy(bf16[4,8,512,256]{3,1,2,0:T(8,128)(2,1)} %bitcast.13) | data formatting | bytes 16777216
  15.1 0.0 copy-done.1
  15.1 0.1 fusion.3
  15.2 0.5 fusion.7
  15.7 0.6 pad_maximum_fusion.1.u_ref
  16.3 0.1 iota_add_fusion
  16.4 0.1 fusion
  16.5 1.0 fusion.6
  17.5 0.7 pad_maximum_fusion.v_ref
  18.2 0.0 copy-done.2
  18.2 0.1 fusion.5
  18.3 0.1 fusion.2
  18.4 0.1 maximum_maximum_fusion.sel_ref
  18.5 0.0 collective-permute-done.follow_ref
  18.5 1.4 copy-done
  19.9 48.9 %front.1 = bf16[32,2,2,16,8,256]{5,4,3,2,1,0:T(8,128)(2,1)} custom-call(s32[16]{0:T(128)} %delays.1, bf16[2,16,512,256]{3,2,1,0:T(8,128)(2,1)} %bitcast.11, bf16[2,16,128,256]{3,2,1,0:T(8,128)(2,1)} %copy-done, f32[16,2,256]{2,1,0:T(2,128)} %pad_maximum_fusion.1.u_ref, f32[16,2,2,256]{3,2,1,0:T(2,128)} %pad_maximum_fusion.v_ref, ...), custom_call_target="tpu_custom_call" | custom-call | tf_op jit(solution)/shard_map/front/pallas_call | solution.py:106
  68.8 8.8 %copy.12 = bf16[8,32,2,2,16,256]{5,4,3,2,1,0:T(8,128)(2,1)} copy(bf16[8,32,2,2,16,256]{5,0,4,3,2,1:T(8,128)(2,1)} %bitcast.12) | data formatting | bytes 16777216 | tf_op jit(solution)/shard_map/transpose | solution.py:260
  77.6 237.8 %cross.1 = f32[2048,4096]{1,0:T(8,128)} custom-call(bf16[8,32,64,256]{3,2,1,0:T(8,128)(2,1)} %bitcast.10, bf16[128,256]{1,0:T(8,128)(2,1)S(1)} %maximum_maximum_fusion.sel_ref), custom_call_target="tpu_custom_call" | custom-call | tf_op jit(solution)/shard_map/cross/pallas_call | solution.py:221
  315.4 23.0 %copy.26 = f32[2048,4096]{1,0:T(8,128)} copy(f32[2048,4096]{1,0:T(8,128)} %cross.1) | data formatting | bytes 67108864
  (5 shorter events, 0.0 us)
Async XLA Ops:
  3.6 14.9 %collective-permute-start = (bf16[2,16,128,256]{3,2,1,0:T(8,128)(2,1)}, bf16[2,16,128,256]{3,2,1,0:T(8,128)(2,1)S(1)}, u32[]{:S(2)}, u32[]{:S(2)}) collective-permute-start(bf16[2,16,128,256]{3,2,1,0:T(8,128)(2,1)} %bitcast.9), channel_id=1, source_target_pairs={{1,0},{2,1},{3,2},{4,3},{5,4},{6,5},{7,6},{9,8},{10,9},{11,10},{12... | collective-permute-start | bytes 6291464 | tf_op jit(solution)/shard_map/ppermute | solution.py:24
  6.3 8.9 %copy-start.1 = (s32[16]{0:T(128)S(1)}, s32[16]{0:T(128)}, u32[]{:S(2)}) copy-start(s32[16]{0:T(128)} %param.10) | copy-start | bytes 196
  6.3 11.9 %copy-start.2 = (s32[64]{0:T(128)S(1)}, s32[64]{0:T(128)}, u32[]{:S(2)}) copy-start(s32[64]{0:T(128)} %param.11) | copy-start | bytes 772
  18.5 1.4 copy-start

commit v3 on v2

--- a/solution.py
+++ b/solution.py
@@ -140,7 +140,7 @@
         return {"station": d // blocks, "cores": lax.rem(d, blocks)}
 
     def remote(step, i):
-        dest = lax.rem(me + i, owners)
+        dest = lax.rem(me + lax.rem(i, groups) * blocks + i // groups, owners)
         return pltpu.make_async_remote_copy(
             src_ref=x_ref.at[step, dest],
             dst_ref=recv.at[step, me],

time: 339 us -> 339 us (level)
  no operation moved by 1% of the time
where the time goes in v3:
time: 339 us; the launch traced here: 338 us
  Pallas kernels  286 us (84%)
  local copies, waits for them, and re-layouts  45.6 us (13%)
    pallas_call x1, Pallas kernels, cross(): pl.pallas_call(functools.partial(cross_kernel, groups, blocks, segs, loca...  237 us
    pallas_call x1, Pallas kernels, front(): pl.pallas_call(functools.partial(front_kernel, segs), grid_spec=pltpu.Pre...  48.9 us
    unnamed x9, local copies, waits for them, and re-layouts  35 us
    transpose x1, local copies, waits for them, and re-layouts, shards(): spectra.transpose(4, 0, 1, 2, 3, 5)  8.82 us
  transfers between devices with their start and end apart: 1, of which 0 were waited for; matrix products, arithmetic and copies ran while one was open for 4% of the time, Pallas kernels for 0%

profile of v3, /device:TPU:15, one launch (start us, length us, event | category | flops | bytes accessed | tf_op | source)
XLA Modules:
  0.0 337.8 jit_solution(6186026998111940896)
XLA Ops:
  0.0 1.7 slice.3
  1.7 1.8 copy.14
  3.6 2.7 collective-permute-start
  6.3 0.0 copy-start.1
  6.3 0.0 copy-start.2
  6.3 8.8 %copy.13 = bf16[4,8,512,256]{3,2,1,0:T(8,128)(2,1)} copy(bf16[4,8,512,256]{3,1,2,0:T(8,128)(2,1)} %bitcast.13) | data formatting | bytes 16777216
  15.1 0.0 copy-done.1
  15.1 0.1 fusion.3
  15.2 0.5 fusion.7
  15.7 0.6 pad_maximum_fusion.1.u_ref
  16.3 0.1 iota_add_fusion
  16.4 0.1 fusion
  16.5 1.0 fusion.6
  17.5 0.7 pad_maximum_fusion.v_ref
  18.2 0.0 copy-done.2
  18.2 0.1 fusion.5
  18.3 0.1 fusion.2
  18.4 0.1 maximum_maximum_fusion.sel_ref
  18.5 0.0 collective-permute-done.follow_ref
  18.5 1.4 copy-done
  19.9 48.9 %front.1 = bf16[32,2,2,16,8,256]{5,4,3,2,1,0:T(8,128)(2,1)} custom-call(s32[16]{0:T(128)} %delays.1, bf16[2,16,512,256]{3,2,1,0:T(8,128)(2,1)} %bitcast.11, bf16[2,16,128,256]{3,2,1,0:T(8,128)(2,1)} %copy-done, f32[16,2,256]{2,1,0:T(2,128)} %pad_maximum_fusion.1.u_ref, f32[16,2,2,256]{3,2,1,0:T(2,128)} %pad_maximum_fusion.v_ref, ...), custom_call_target="tpu_custom_call" | custom-call | tf_op jit(solution)/shard_map/front/pallas_call | solution.py:106
  68.8 8.8 %copy.12 = bf16[8,32,2,2,16,256]{5,4,3,2,1,0:T(8,128)(2,1)} copy(bf16[8,32,2,2,16,256]{5,0,4,3,2,1:T(8,128)(2,1)} %bitcast.12) | data formatting | bytes 16777216 | tf_op jit(solution)/shard_map/transpose | solution.py:260
  77.6 237.2 %cross.1 = f32[2048,4096]{1,0:T(8,128)} custom-call(bf16[8,32,64,256]{3,2,1,0:T(8,128)(2,1)} %bitcast.10, bf16[128,256]{1,0:T(8,128)(2,1)S(1)} %maximum_maximum_fusion.sel_ref), custom_call_target="tpu_custom_call" | custom-call | tf_op jit(solution)/shard_map/cross/pallas_call | solution.py:221
  314.8 23.0 %copy.26 = f32[2048,4096]{1,0:T(8,128)} copy(f32[2048,4096]{1,0:T(8,128)} %cross.1) | data formatting | bytes 67108864
  (5 shorter events, 0.0 us)
Async XLA Ops:
  3.6 14.9 %collective-permute-start = (bf16[2,16,128,256]{3,2,1,0:T(8,128)(2,1)}, bf16[2,16,128,256]{3,2,1,0:T(8,128)(2,1)S(1)}, u32[]{:S(2)}, u32[]{:S(2)}) collective-permute-start(bf16[2,16,128,256]{3,2,1,0:T(8,128)(2,1)} %bitcast.9), channel_id=1, source_target_pairs={{1,0},{2,1},{3,2},{4,3},{5,4},{6,5},{7,6},{9,8},{10,9},{11,10},{12... | collective-permute-start | bytes 6291464 | tf_op jit(solution)/shard_map/ppermute | solution.py:24
  6.3 8.9 %copy-start.1 = (s32[16]{0:T(128)S(1)}, s32[16]{0:T(128)}, u32[]{:S(2)}) copy-start(s32[16]{0:T(128)} %param.10) | copy-start | bytes 196
  6.3 11.9 %copy-start.2 = (s32[64]{0:T(128)S(1)}, s32[64]{0:T(128)}, u32[]{:S(2)}) copy-start(s32[64]{0:T(128)} %param.11) | copy-start | bytes 772
  18.5 1.4 copy-start

commit v4 on v2

--- a/solution.py
+++ b/solution.py
@@ -129,67 +129,13 @@
     )(delays, samples, following, u, v, jnp.asarray(table), jnp.asarray(dft_table(NCH, 1.0 / 256.0)), gh, gl)
 
 
-def cross_kernel(groups, blocks, segs, local_rows, x_ref, sel_ref, o_ref, recv, wide, packed, send_sem, recv_sem, own_sem):
-    q = pl.program_id(0)
-    count = pl.num_programs(0)
-    owners = groups * blocks
+def products(groups, blocks, segs, local_rows, arrived, sel_ref, o_ref, wide, packed):
     total_segs = blocks * segs
-    me = lax.axis_index("station") * blocks + lax.axis_index("cores")
-
-    def coords(d):
-        return {"station": d // blocks, "cores": lax.rem(d, blocks)}
-
-    def remote(step, i):
-        dest = lax.rem(me + i, owners)
-        return pltpu.make_async_remote_copy(
-            src_ref=x_ref.at[step, dest],
-            dst_ref=recv.at[step, me],
-            send_sem=send_sem.at[step],
-            recv_sem=recv_sem.at[step],
-            device_id=coords(dest),
-            device_id_type=pl.DeviceIdType.MESH,
-        )
-
-    def own(step):
-        return pltpu.make_async_copy(x_ref.at[step, me], recv.at[step, me], own_sem.at[step])
-
-    @pl.when(q == 0)
-    def _():
-        barrier = pltpu.get_barrier_semaphore()
-
-        @pl.loop(1, owners)
-        def _(i):
-            pl.semaphore_signal(
-                barrier, inc=1, device_id=coords(lax.rem(me + i, owners)), device_id_type=pl.DeviceIdType.MESH
-            )
-
-        pl.semaphore_wait(barrier, owners - 1)
-
-        @pl.loop(0, x_ref.shape[0])
-        def _(step):
-            own(step).start()
-
-            @pl.loop(1, owners)
-            def _(i):
-                remote(step, i).start()
-
-    own(q).wait()
-
-    others = recv.at[q, pl.ds(0, owners - 1)]
-    pltpu.make_async_copy(others, others, recv_sem.at[q]).wait()
-
-    @pl.when(q == count - 1)
-    def _():
-        @pl.loop(0, x_ref.shape[0])
-        def _(step):
-            gone = recv.at[step, pl.ds(0, owners - 1)]
-            pltpu.make_async_copy(gone, gone, send_sem.at[step]).wait()
-
     for g in range(total_segs):
         c, s = g // segs, g % segs
         x = jnp.concatenate(
             [
-                recv[q, st * blocks + c, (p * segs + s) * local_rows : (p * segs + s + 1) * local_rows, :]
+                arrived[st * blocks + c, (p * segs + s) * local_rows : (p * segs + s + 1) * local_rows, :]
                 for p in range(2)
                 for st in range(groups)
             ],
@@ -215,18 +161,105 @@
             o_ref[pl.ds(pl.multiple_of(block * 8, 8), 8), j * 128 : (j + 1) * 128] = jnp.where(left, even, odd)
 
 
+def cross_kernel(groups, blocks, segs, local_rows, x_ref, sel_ref, o_ref, last_ref, recv, wide, packed, send_sem, recv_sem, own_sem):
+    q = pl.program_id(0)
+    count = pl.num_programs(0)
+    owners = groups * blocks
+    me = lax.axis_index("station") * blocks + lax.axis_index("cores")
+
+    def coords(d):
+        return {"station": d // blocks, "cores": lax.rem(d, blocks)}
+
+    def remote(step, i):
+        dest = lax.rem(me + i, owners)
+        return pltpu.make_async_remote_copy(
+            src_ref=x_ref.at[step, dest],
+            dst_ref=recv.at[step, me],
+            send_sem=send_sem.at[step],
+            recv_sem=recv_sem.at[step],
+            device_id=coords(dest),
+            device_id_type=pl.DeviceIdType.MESH,
+        )
+
+    def own(step):
+        return pltpu.make_async_copy(x_ref.at[step, me], recv.at[step, me], own_sem.at[step])
+
+    @pl.when(q == 0)
+    def _():
+        barrier = pltpu.get_barrier_semaphore()
+
+        @pl.loop(1, owners)
+        def _(i):
+            pl.semaphore_signal(
+                barrier, inc=1, device_id=coords(lax.rem(me + i, owners)), device_id_type=pl.DeviceIdType.MESH
+            )
+
+        pl.semaphore_wait(barrier, owners - 1)
+
+        @pl.loop(0, x_ref.shape[0])
+        def _(step):
+            own(step).start()
+
+            @pl.loop(1, owners)
+            def _(i):
+                remote(step, i).start()
+
+    own(q).wait()
+
+    others = recv.at[q, pl.ds(0, owners - 1)]
+    pltpu.make_async_copy(others, others, recv_sem.at[q]).wait()
+
+    @pl.when(q == count - 1)
+    def _():
+        @pl.loop(0, x_ref.shape[0])
+        def _(step):
+            gone = recv.at[step, pl.ds(0, owners - 1)]
+            pltpu.make_async_copy(gone, gone, send_sem.at[step]).wait()
+
+    @pl.when(q < count - 1)
+    def _():
+        products(groups, blocks, segs, local_rows, recv.at[q], sel_ref, o_ref, wide, packed)
+
+    @pl.when(q == count - 1)
+    def _():
+        pltpu.sync_copy(recv.at[q], last_ref)
+
+
+def last_kernel(groups, blocks, segs, local_rows, x_ref, sel_ref, done_ref, o_ref, tile, wide, packed, sems, tile_sem):
+    count = done_ref.shape[0] // ROOT
+
+    def moved(step):
+        rows = pl.ds(step * ROOT, ROOT)
+        return pltpu.make_async_copy(done_ref.at[rows], o_ref.at[rows], sems.at[step])
+
+    for step in range(count):
+        moved(step).start()
+    products(groups, blocks, segs, local_rows, x_ref, sel_ref, tile, wide, packed)
+    final = pltpu.make_async_copy(tile, o_ref.at[pl.ds(count * ROOT, ROOT)], tile_sem)
+    final.start()
+    for step in range(count):
+        moved(step).wait()
+    final.wait()
+
+
 def cross(x, sel, groups, blocks, segs, local_rows):
     owned = x.shape[0]
     total_segs = blocks * segs
-    return pl.pallas_call(
+    done, last = pl.pallas_call(
         functools.partial(cross_kernel, groups, blocks, segs, local_rows),
         grid=(owned,),
         in_specs=[
             pl.BlockSpec(memory_space=pl.ANY),
             pl.BlockSpec((2 * S, 4 * S), lambda q: (0, 0)),
         ],
-        out_specs=pl.BlockSpec((ROOT, S * S), lambda q: (q, 0)),
-        out_shape=jax.ShapeDtypeStruct((owned * ROOT, S * S), F32),
+        out_specs=[
+            pl.BlockSpec((ROOT, S * S), lambda q: (jnp.minimum(q, owned - 2), 0)),
+            pl.BlockSpec(memory_space=pl.ANY),
+        ],
+        out_shape=[
+            jax.ShapeDtypeStruct(((owned - 1) * ROOT, S * S), F32),
+            jax.ShapeDtypeStruct(x.shape[1:], BF16),
+        ],
         scratch_shapes=[
             pltpu.VMEM(x.shape, BF16),
             pltpu.VMEM((2 * total_segs * ROOT, 128), F32),
@@ -240,6 +273,25 @@
         ),
         name="cross",
     )(x, sel)
+    return pl.pallas_call(
+        functools.partial(last_kernel, groups, blocks, segs, local_rows),
+        in_specs=[
+            pl.BlockSpec(memory_space=pltpu.VMEM),
+            pl.BlockSpec(memory_space=pltpu.VMEM),
+            pl.BlockSpec(memory_space=pl.ANY),
+        ],
+        out_specs=pl.BlockSpec(memory_space=pl.ANY),
+        out_shape=jax.ShapeDtypeStruct((owned * ROOT, S * S), F32),
+        scratch_shapes=[
+            pltpu.VMEM((ROOT, S * S), F32),
+            pltpu.VMEM((2 * total_segs * ROOT, 128), F32),
+            pltpu.VMEM((8 * S, 128), F32),
+            pltpu.SemaphoreType.DMA((owned - 1,)),
+            pltpu.SemaphoreType.DMA,
+        ],
+        compiler_params=pltpu.CompilerParams(vmem_limit_bytes=48 * 1024 * 1024),
+        name="last",
+    )(last, sel, done)
 
 
 def shards(samples, delays, fringe_rate, station_of_row):

time: 339 us -> 1190 us (3.51)
  Pallas kernels: 287 us -> 1160 us
  local copies, waits for them, and re-layouts: 45.6 us -> 22.6 us
    pallas_call x0 -> x1, Pallas kernels: none -> 891 us  [cross(): pl.pallas_call(functools.partial(last_kernel, groups, blocks, segs, local...]
    unnamed x9 -> x8, local copies, waits for them, and re-layouts: 35 us -> 12 us
    pallas_call x1, Pallas kernels: 238 us -> 222 us  [cross(): pl.pallas_call(functools.partial(cross_kernel, groups, blocks, segs, loca...]
  transfers between devices with their start and end apart: 1 -> 1, of which waited for: 0 -> 0; matrix products, arithmetic and copies ran while one was open for 4% -> 1% of each run, Pallas kernels for 0% -> 0%
where the time goes in v4:
time: 1190 us
  Pallas kernels  1160 us (97%)
  local copies, waits for them, and re-layouts  22.6 us (2%)
    pallas_call x1, Pallas kernels, cross(): pl.pallas_call(functools.partial(last_kernel, groups, blocks, segs, local...  891 us
    pallas_call x1, Pallas kernels, cross(): pl.pallas_call(functools.partial(cross_kernel, groups, blocks, segs, loca...  222 us
    pallas_call x1, Pallas kernels, front(): pl.pallas_call(functools.partial(front_kernel, segs), grid_spec=pltpu.Pre...  48.9 us
  transfers between devices with their start and end apart: 1, of which 0 were waited for; matrix products, arithmetic and copies ran while one was open for 1% of the time, Pallas kernels for 0%

profile of v4, /device:TPU:15, one launch (start us, length us, event | category | flops | bytes accessed | tf_op | source)
XLA Modules:
  0.0 1189.9 jit_solution(2255775275492129087)
XLA Ops:
  0.0 1.7 slice.3
  1.7 1.8 copy.14
  3.6 2.7 collective-permute-start
  6.3 0.0 copy-start.1
  6.3 0.0 copy-start.2
  6.3 8.8 copy.13
  15.1 0.0 copy-done.1
  15.2 0.1 fusion.3
  15.2 0.5 fusion.7
  15.7 0.6 pad_maximum_fusion.1.u_ref
  16.4 0.1 iota_add_fusion
  16.4 0.1 fusion
  16.5 1.0 fusion.6
  17.5 0.7 pad_maximum_fusion.v_ref
  18.2 0.0 copy-done.2
  18.2 0.1 fusion.5
  18.3 0.1 fusion.2
  18.4 0.1 maximum_maximum_fusion.sel_ref
  18.5 0.0 collective-permute-done.follow_ref
  18.5 1.3 copy-done
  19.9 48.9 %front.1 = bf16[32,2,2,16,8,256]{5,4,3,2,1,0:T(8,128)(2,1)} custom-call(s32[16]{0:T(128)} %delays.1, bf16[2,16,512,256]{3,2,1,0:T(8,128)(2,1)} %bitcast.10, bf16[2,16,128,256]{3,2,1,0:T(8,128)(2,1)} %copy-done, f32[16,2,256]{2,1,0:T(2,128)} %pad_maximum_fusion.1.u_ref, f32[16,2,2,256]{3,2,1,0:T(2,128)} %pad_maximum_fusion.v_ref, ...), custom_call_target="tpu_custom_call" | custom-call | tf_op jit(solution)/shard_map/front/pallas_call | solution.py:106
  68.8 8.8 copy.12
  77.6 221.6 %cross.1 = (f32[1792,4096]{1,0:T(8,128)}, bf16[32,64,256]{2,1,0:T(8,128)(2,1)S(1)}) custom-call(bf16[8,32,64,256]{3,2,1,0:T(8,128)(2,1)} %bitcast.12, bf16[128,256]{1,0:T(8,128)(2,1)S(1)} %maximum_maximum_fusion.sel_ref), custom_call_target="tpu_custom_call" | custom-call | tf_op jit(solution)/shard_map/cross/pallas_call | solution.py:248
  299.3 890.6 %last.1 = f32[2048,4096]{1,0:T(8,128)} custom-call(bf16[32,64,256]{2,1,0:T(8,128)(2,1)S(1)} %get-tuple-element.7.x_ref, bf16[128,256]{1,0:T(8,128)(2,1)S(1)} %maximum_maximum_fusion.sel_ref, f32[1792,4096]{1,0:T(8,128)} %get-tuple-element.8.done_ref), custom_call_target="tpu_custom_call" | custom-call | tf_op jit(solution)/shard_map/last/pallas_call | solution.py:276
  (5 shorter events, 0.0 us)
Async XLA Ops:
  3.6 14.9 %collective-permute-start = (bf16[2,16,128,256]{3,2,1,0:T(8,128)(2,1)}, bf16[2,16,128,256]{3,2,1,0:T(8,128)(2,1)S(1)}, u32[]{:S(2)}, u32[]{:S(2)}) collective-permute-start(bf16[2,16,128,256]{3,2,1,0:T(8,128)(2,1)} %bitcast.9), channel_id=1, source_target_pairs={{1,0},{2,1},{3,2},{4,3},{5,4},{6,5},{7,6},{9,8},{10,9},{11,10},{12... | collective-permute-start | bytes 6291464 | tf_op jit(solution)/shard_map/ppermute | solution.py:24
  6.3 8.9 copy-start.1
  6.3 11.9 %copy-start.2 = (s32[64]{0:T(128)S(1)}, s32[64]{0:T(128)}, u32[]{:S(2)}) copy-start(s32[64]{0:T(128)} %param.11) | copy-start | bytes 772
  18.5 1.4 copy-start
